TPU v7x, 32 devices: a whole 2x2x4 slice. The times are simulated.
32 devices in a mesh: row: 8 (over z, x), col: 4 (over y, core).
Axes of the slice: x: 2, y: 2, z: 4, core: 2. Of those that a mesh axis runs over, the one named last changes fastest.
Arguments:
- patches: bfloat16 [16384, 1024], P('row', 'col'), may hold values from -16 to 16
- w_query: bfloat16 [1024, 1024], P('row', 'col'), may hold values from -0.1875 to 0.1875
- w_key: bfloat16 [1024, 1024], P('row', 'col'), may hold values from -0.1875 to 0.1875
- w_value: bfloat16 [1024, 1024], P('row', 'col'), may hold values from -0.1875 to 0.1875
- w_out: bfloat16 [1024, 1024], P('col', 'row'), may hold values from -2 to 2
- w_gate: bfloat16 [1024, 2816], P('row', 'col'), may hold values from -0.1875 to 0.1875
- w_up: bfloat16 [1024, 2816], P('row', 'col'), may hold values from -0.1875 to 0.1875
- w_down: bfloat16 [2816, 1024], P('col', 'row'), may hold values from -0.109375 to 0.109375
- gain_attn: bfloat16 [1024], P('row'), may hold values from 0.5 to 1.5
- gain_mlp: bfloat16 [1024], P('row'), may hold values from 0.5 to 1.5
- lengths: int32 [16], P('row'), may hold values from 256 to 1024, as said below
- cotangent: bfloat16 [16384, 1024], P('row', 'col'), may hold values from -6 to 6
Outputs:
- output: bfloat16 [16384, 1024], P('row', 'col')
- grad_patches: float32 [16384, 1024], P('row', 'col')
- grad_query: float32 [1024, 1024], P('row', 'col')
- grad_key: float32 [1024, 1024], P('row', 'col')
- grad_value: float32 [1024, 1024], P('row', 'col')
- grad_out: float32 [1024, 1024], P('col', 'row')
- grad_gate: float32 [1024, 2816], P('row', 'col')
- grad_up: float32 [1024, 2816], P('row', 'col')
- grad_down: float32 [2816, 1024], P('col', 'row')
- grad_gain_attn: float32 [1024], P('row')
- grad_gain_mlp: float32 [1024], P('row')
Inputs may be any that keep to these rules, and one draw needn't show every extreme that they name: Each sequence's valid slots are its first lengths[s]; every draw has a sequence with all 1024 slots valid and one with 256.
All inputs are finite; a program needn't handle non-finite values.
Results may differ from a plain program's by a relative error of at most 0.012.
The roundings to bfloat16 on the way count: a program that leaves them out, or rounds other values in their place, can miss the bound.
Values may be sent and summed in bfloat16 or wider, within the bound.
No kernel may reach another device: no remote copies, remote signals or barrier semaphores. Data moves between devices by JAX's collectives and lax.ppermute only.
A program may use at most 192 MiB of HBM per device.

v0:
```python
import jax
import jax.numpy as jnp
from jax import lax
from jax.sharding import PartitionSpec as P

HEAD_DIM = 64
EPSILON = 1e-06
MASKED = -1000000000.0


def times_trans(left, right):
    return lax.dot_general(
        left, right, (((1,), (1,)), ((), ())), preferred_element_type=jnp.float32
    )


def contract_rows(left, right):
    return lax.dot_general(
        left, right, (((0,), (0,)), ((), ())), preferred_element_type=jnp.float32
    )


def shards(
    patches,
    w_query,
    w_key,
    w_value,
    w_out,
    w_gate,
    w_up,
    w_down,
    gain_attn,
    gain_mlp,
    lengths,
    cotangent,
):
    slab = patches.shape[1]
    width = slab * lax.axis_size("col")
    col_start = lax.axis_index("col") * slab
    micro = lengths.shape[0]
    seq = patches.shape[0] // micro
    heads_here = w_query.shape[1] // HEAD_DIM
    scale = HEAD_DIM ** (-0.5)
    block = min(512, seq)
    positions = lax.iota(jnp.int32, seq)

    def fetch():
        return (
            lax.all_gather(w_query, "row", axis=0, tiled=True),
            lax.all_gather(w_key, "row", axis=0, tiled=True),
            lax.all_gather(w_value, "row", axis=0, tiled=True),
            lax.all_gather(w_out, "row", axis=1, tiled=True),
            lax.all_gather(w_gate, "row", axis=0, tiled=True),
            lax.all_gather(w_up, "row", axis=0, tiled=True),
            lax.all_gather(w_down, "row", axis=1, tiled=True),
            lax.all_gather(gain_attn, "row", axis=0, tiled=True),
            lax.all_gather(gain_mlp, "row", axis=0, tiled=True),
        )

    def to_full(values_own):
        return lax.all_gather(values_own, "col", axis=1, tiled=True)

    def reduce_cols(partial_value):
        return lax.psum_scatter(partial_value, "col", scatter_dimension=1, tiled=True)

    def norm_forward(rows_own, gain_whole):
        total = lax.psum(jnp.sum(rows_own * rows_own, axis=1), "col")
        rstd = lax.rsqrt(total / width + EPSILON)
        gain_own = lax.dynamic_slice_in_dim(gain_whole, col_start, slab).astype(jnp.float32)
        normed = (rows_own * rstd[:, None] * gain_own).astype(jnp.bfloat16)
        return (normed, rstd, gain_own)

    def norm_backward(grad_partial, rows_own, rstd, gain_own):
        grad_normed = reduce_cols(grad_partial)
        weighted = grad_normed * gain_own
        gain_piece = jnp.sum(grad_normed * rows_own * rstd[:, None], axis=0)
        gain_whole = lax.dynamic_update_slice_in_dim(
            jnp.zeros((width,), jnp.float32), gain_piece, col_start, 0
        )
        stat, gain_grad = lax.psum((jnp.sum(weighted * rows_own, axis=1), gain_whole), "col")
        grad_rows = (
            rstd[:, None] * weighted - rows_own * (rstd * rstd * rstd * stat / width)[:, None]
        )
        return (grad_rows, gain_grad)

    def split_heads(tensor):
        return jnp.transpose(tensor.reshape(seq, heads_here, HEAD_DIM), (1, 0, 2))

    def join_heads(tensor):
        return jnp.transpose(tensor, (1, 0, 2)).reshape(seq, heads_here * HEAD_DIM)

    def block_scores(query_h, key_h, first_row, last_row, length):
        raw = times_trans(query_h[first_row:last_row], key_h[:last_row]) * scale
        keep = (positions[None, :last_row] <= positions[first_row:last_row, None]) & (
            positions[None, :last_row] < length
        )
        return jnp.where(keep, raw, MASKED)

    outputs = []
    input_grads = []
    totals = None
    for batch in range(micro):
        first_slot = batch * seq
        weights_now = fetch()
        (
            query_full,
            key_full,
            value_full,
            out_full,
            gate_full,
            up_full,
            down_full,
            attn_gain,
            mlp_gain,
        ) = weights_now
        rows_own = patches[first_slot : first_slot + seq].astype(jnp.float32)
        length = lengths[batch]
        valid = (positions < length)[:, None]
        normed_own, rstd_one, gain_one = norm_forward(rows_own, attn_gain)
        normed_one = to_full(normed_own)
        queries = split_heads(
            jnp.dot(normed_one, query_full, preferred_element_type=jnp.float32).astype(jnp.bfloat16)
        )
        keys_all = split_heads(
            jnp.dot(normed_one, key_full, preferred_element_type=jnp.float32).astype(jnp.bfloat16)
        )
        values_all = split_heads(
            jnp.dot(normed_one, value_full, preferred_element_type=jnp.float32).astype(jnp.bfloat16)
        )

        def attend_per_head(operands):
            query_h, key_h, value_h = operands
            pieces = []
            totals = []
            for index in range(seq // block):
                first_row = index * block
                last_row = first_row + block
                scores = block_scores(query_h, key_h, first_row, last_row, length)
                peak = jnp.max(scores, axis=1, keepdims=True)
                expo = jnp.exp(scores - peak)
                denom = jnp.sum(expo, axis=1, keepdims=True)
                probs = (expo / denom).astype(jnp.bfloat16)
                pieces.append(
                    jnp.dot(probs, value_h[:last_row], preferred_element_type=jnp.float32)
                )
                totals.append((peak + jnp.log(denom))[:, 0])
            return (jnp.concatenate(pieces, axis=0), jnp.concatenate(totals, axis=0))

        attended, logsum = lax.map(attend_per_head, (queries, keys_all, values_all))
        attended = join_heads(attended).astype(jnp.bfloat16)
        hstate = rows_own + reduce_cols(
            jnp.dot(attended, out_full, preferred_element_type=jnp.float32)
        )
        normed_own_two, rstd_two, gain_two = norm_forward(hstate, mlp_gain)
        normed_two = to_full(normed_own_two)
        gate = jnp.dot(normed_two, gate_full, preferred_element_type=jnp.float32)
        upward = jnp.dot(normed_two, up_full, preferred_element_type=jnp.float32)
        sigmoid_gate = jax.nn.sigmoid(gate)
        activated = gate * sigmoid_gate
        hidden = (activated * upward).astype(jnp.bfloat16)
        mixed = reduce_cols(jnp.dot(hidden, down_full, preferred_element_type=jnp.float32))
        outputs.append(jnp.where(valid, hstate + mixed, 0.0).astype(jnp.bfloat16))
        weights_back = fetch()
        (
            query_full,
            key_full,
            value_full,
            out_full,
            gate_full,
            up_full,
            down_full,
            attn_gain,
            mlp_gain,
        ) = weights_back
        grad_mixed = jnp.where(
            valid, cotangent[first_slot : first_slot + seq], jnp.zeros((), jnp.bfloat16)
        )
        grad_mixed_full = to_full(grad_mixed)
        grad_hidden = times_trans(grad_mixed_full, down_full)
        down_grad = contract_rows(hidden, grad_mixed_full)
        grad_gate_act = (
            grad_hidden * upward * sigmoid_gate * (1.0 + gate * (1.0 - sigmoid_gate))
        ).astype(jnp.bfloat16)
        grad_up_act = (grad_hidden * activated).astype(jnp.bfloat16)
        gate_grad = contract_rows(normed_two, grad_gate_act)
        up_grad = contract_rows(normed_two, grad_up_act)
        grad_normed_two = times_trans(grad_gate_act, gate_full) + times_trans(grad_up_act, up_full)
        grad_norm_two, mlp_gain_grad = norm_backward(grad_normed_two, hstate, rstd_two, gain_two)
        grad_hstate = grad_mixed.astype(jnp.float32) + grad_norm_two
        grad_branch = to_full(grad_hstate.astype(jnp.bfloat16))
        out_grad = contract_rows(attended, grad_branch)
        grad_attended = split_heads(times_trans(grad_branch, out_full).astype(jnp.bfloat16))

        def per_head(operands):
            query_h, key_h, value_h, grad_h, logsum_h = operands
            query_parts = []
            key_grad = jnp.zeros((seq, HEAD_DIM), jnp.float32)
            value_grad = jnp.zeros((seq, HEAD_DIM), jnp.float32)
            for index in range(seq // block):
                first_row = index * block
                last_row = first_row + block
                scores = block_scores(query_h, key_h, first_row, last_row, length)
                probs = jnp.exp(scores - logsum_h[first_row:last_row, None])
                rounded = probs.astype(jnp.bfloat16)
                grad_probs = times_trans(grad_h[first_row:last_row], value_h[:last_row])
                inner = jnp.sum(probs * grad_probs, axis=1, keepdims=True)
                grad_scores = (probs * (grad_probs - inner)).astype(jnp.bfloat16)
                query_parts.append(
                    jnp.dot(grad_scores, key_h[:last_row], preferred_element_type=jnp.float32)
                    * scale
                )
                key_grad = key_grad.at[:last_row].add(
                    contract_rows(grad_scores, query_h[first_row:last_row]) * scale
                )
                value_grad = value_grad.at[:last_row].add(
                    contract_rows(rounded, grad_h[first_row:last_row])
                )
            query_grad = jnp.concatenate(query_parts, axis=0)
            return (
                query_grad.astype(jnp.bfloat16),
                key_grad.astype(jnp.bfloat16),
                value_grad.astype(jnp.bfloat16),
            )

        grad_queries, grad_keys, grad_values = lax.map(
            per_head, (queries, keys_all, values_all, grad_attended, logsum)
        )
        grad_queries = join_heads(grad_queries)
        grad_keys = join_heads(grad_keys)
        grad_values = join_heads(grad_values)
        query_grad = contract_rows(normed_one, grad_queries)
        key_grad = contract_rows(normed_one, grad_keys)
        value_grad = contract_rows(normed_one, grad_values)
        grad_normed_one = (
            times_trans(grad_queries, query_full)
            + times_trans(grad_keys, key_full)
            + times_trans(grad_values, value_full)
        )
        grad_norm_one, attn_gain_grad = norm_backward(grad_normed_one, rows_own, rstd_one, gain_one)
        input_grads.append(grad_hstate + grad_norm_one)
        local_terms = (
            query_grad,
            key_grad,
            value_grad,
            out_grad,
            gate_grad,
            up_grad,
            down_grad,
            attn_gain_grad,
            mlp_gain_grad,
        )
        reduced = (
            lax.psum_scatter(local_terms[0], "row", scatter_dimension=0, tiled=True),
            lax.psum_scatter(local_terms[1], "row", scatter_dimension=0, tiled=True),
            lax.psum_scatter(local_terms[2], "row", scatter_dimension=0, tiled=True),
            lax.psum_scatter(local_terms[3], "row", scatter_dimension=1, tiled=True),
            lax.psum_scatter(local_terms[4], "row", scatter_dimension=0, tiled=True),
            lax.psum_scatter(local_terms[5], "row", scatter_dimension=0, tiled=True),
            lax.psum_scatter(local_terms[6], "row", scatter_dimension=1, tiled=True),
            lax.psum_scatter(local_terms[7], "row", scatter_dimension=0, tiled=True),
            lax.psum_scatter(local_terms[8], "row", scatter_dimension=0, tiled=True),
        )
        totals = reduced if totals is None else jax.tree.map(jnp.add, totals, reduced)
    return (
        jnp.concatenate(outputs, axis=0),
        jnp.concatenate(input_grads, axis=0),
        totals[0],
        totals[1],
        totals[2],
        totals[3],
        totals[4],
        totals[5],
        totals[6],
        totals[7],
        totals[8],
    )


def solution(mesh):
    placed = (
        P("row", "col"),
        P("row", "col"),
        P("row", "col"),
        P("row", "col"),
        P("col", "row"),
        P("row", "col"),
        P("row", "col"),
        P("col", "row"),
        P("row"),
        P("row"),
        P("row"),
        P("row", "col"),
    )
    return jax.shard_map(
        shards,
        mesh=mesh,
        in_specs=placed,
        out_specs=(
            P("row", "col"),
            P("row", "col"),
            P("row", "col"),
            P("row", "col"),
            P("row", "col"),
            P("col", "row"),
            P("row", "col"),
            P("row", "col"),
            P("col", "row"),
            P("row"),
            P("row"),
        ),
        check_vma=False,
    )
```

profile of v0, /device:TPU:0, one launch (start us, length us, event | category | flops | bytes accessed | tf_op | source)
XLA Modules:
  0.0 1450.2 jit_solution(8379913101905790760)
XLA Ops:
  8.1 22.3 %all-gather = bf16[8,1,128]{2,1,0:T(2,128)(2,1)S(1)} all-gather(bf16[1,1,128]{2,1,0:T(2,128)(2,1)} %bitcast.471), channel_id=1, replica_groups=mesh['row'=8,'col'=4] {'row'}, dimensions={0}, use_global_device_ids=true | all-gather | bytes 2304 | tf_op jit(solution)/shard_map/all_gather | solution.py:56
  32.1 5.7 all-reduce.10
  41.3 31.7 %all_gather.36 = bf16[1024,256]{1,0:T(8,128)(2,1)S(1)} all-gather(bf16[128,256]{1,0:T(8,128)(2,1)S(1)} %copy-done.36), channel_id=1, replica_groups=mesh['row'=8,'col'=4] {'row'}, dimensions={0}, use_global_device_ids=true | all-gather | bytes 589824 | tf_op jit(solution)/shard_map/all_gather | solution.py:49
  73.0 31.4 %all_gather.37 = bf16[1024,256]{1,0:T(8,128)(2,1)S(1)} all-gather(bf16[128,256]{1,0:T(8,128)(2,1)S(1)} %copy-done.37), channel_id=1, replica_groups=mesh['row'=8,'col'=4] {'row'}, dimensions={0}, use_global_device_ids=true | all-gather | bytes 589824 | tf_op jit(solution)/shard_map/all_gather | solution.py:50
  104.5 33.4 %all_gather.38 = bf16[1024,256]{1,0:T(8,128)(2,1)} all-gather(bf16[128,256]{1,0:T(8,128)(2,1)S(1)} %copy-done.38), channel_id=1, replica_groups=mesh['row'=8,'col'=4] {'row'}, dimensions={0}, use_global_device_ids=true | all-gather | bytes 589824 | tf_op jit(solution)/shard_map/all_gather | solution.py:51
  138.5 28.1 %all_gather.39 = bf16[256,1024]{1,0:T(8,128)(2,1)} all-gather(bf16[256,128]{1,0:T(8,128)(2,1)S(1)} %copy-done.39), channel_id=1, replica_groups=mesh['row'=8,'col'=4] {'row'}, dimensions={1}, use_global_device_ids=true | all-gather | bytes 589824 | tf_op jit(solution)/shard_map/all_gather | solution.py:52
  179.1 34.7 %while.74 = (s32[]{:T(128)}, bf16[4,1024,64]{1,2,0:T(8,128)(2,1)}, f32[4,1024]{1,0:T(4,128)S(1)}, s32[1024]{0:T(1024)S(1)}, s32[]{:T(128)}, /*index=5*/bf16[4,10...) while((s32[]{:T(128)}, bf16[4,1024,64]{1,2,0:T(8,128)(2,1)}, ...), condition=%wide.region_7.8_spmd.clone, body=%wide.region_2.7_spmd.clone.sunk | while | flops 209454592 | bytes 10959497 | solution.py:149
  213.8 3.9 fusion.135
  231.3 34.8 %while.75 = (s32[]{:T(128)}, bf16[4,1024,64]{1,2,0:T(8,128)(2,1)}, f32[4,1024]{1,0:T(4,128)S(1)}, s32[1024]{0:T(1024)S(1)}, s32[]{:T(128)}, /*index=5*/bf16[4,10...) while((s32[]{:T(128)}, bf16[4,1024,64]{1,2,0:T(8,128)(2,1)}, ...), condition=%wide.region_19.20_spmd.clone, body=%wide.region_14.19_spmd.clone.sunk | while | flops 209454592 | bytes 10959497 | solution.py:149
  266.1 3.9 fusion.139
  270.7 16.3 %all-gather.1 = bf16[8,1,128]{2,1,0:T(2,128)(2,1)S(1)} all-gather(bf16[1,1,128]{2,1,0:T(2,128)(2,1)S(1)} %bitcast.472), channel_id=1, replica_groups=mesh['row'=8,'col'=4] {'row'}, dimensions={0}, use_global_device_ids=true | all-gather | bytes 2304 | tf_op jit(solution)/shard_map/all_gather | solution.py:57
  287.1 25.6 %reduce-scatter.20.cloned.1.call-done = f32[1024,256]{1,0:T(8,128)} async-done(((f32[1024,1024]{1,0:T(8,128)}), f32[1024,256]{1,0:T(8,128)}) %reduce-scatter.20.cloned.1.call-update) | async-done | bytes 1048592 | tf_op jit(solution)/shard_map/reduce_scatter | solution.py:64
  314.6 6.0 all-reduce.9
  326.3 19.3 %all-gather.16.cloned.1.call-done = bf16[1024,1024]{1,0:T(8,128)(2,1)} async-done(((bf16[1024,256]{1,0:T(8,128)(2,1)}), bf16[1024,1024]{1,0:T(8,128)(2,1)}) %all-gather.16.cloned.1.call-update) | async-done | bytes 2097168 | tf_op jit(solution)/shard_map/all_gather | solution.py:61
  345.6 5.2 fusion.136
  350.8 39.8 %all-gather.20.cloned.1.call-done = bf16[1024,704]{0,1:T(8,128)(2,1)} async-done(((bf16[128,704]{0,1:T(8,128)(2,1)}), bf16[1024,704]{0,1:T(8,128)(2,1)}) %all-gather.20.cloned.1.call-update) | async-done | bytes 1441808 | tf_op jit(solution)/shard_map/all_gather | solution.py:54
  390.7 5.3 fusion.137
  395.9 38.2 %all-gather.22.cloned.1.call-done = bf16[704,1024]{1,0:T(8,128)(2,1)} async-done(((bf16[704,128]{1,0:T(8,128)(2,1)}), bf16[704,1024]{1,0:T(8,128)(2,1)}) %all-gather.22.cloned.1.call-update) | async-done | bytes 1441808 | tf_op jit(solution)/shard_map/all_gather | solution.py:55
  434.1 22.5 %all-gather.28.cloned.1.call-done = bf16[1024,1024]{1,0:T(8,128)(2,1)} async-done(((bf16[1024,256]{1,0:T(8,128)(2,1)}), bf16[1024,1024]{1,0:T(8,128)(2,1)}) %all-gather.28.cloned.1.call-update) | async-done | bytes 2097168 | tf_op jit(solution)/shard_map/all_gather | solution.py:61
  456.6 7.6 multiply_convert_fusion.6
  466.7 3.9 convolution_add_fusion.3
  470.7 44.5 %reduce-scatter.24.cloned.1.call-done = f32[1024,256]{1,0:T(8,128)} async-done(((f32[1024,1024]{1,0:T(8,128)}), f32[1024,256]{1,0:T(8,128)}) %reduce-scatter.24.cloned.1.call-update) | async-done | bytes 1048592 | tf_op jit(solution)/shard_map/reduce_scatter | solution.py:64
  519.2 21.7 %all-gather.26.cloned.1.call-done = bf16[1024,1024]{1,0:T(8,128)(2,1)} async-done(((bf16[1024,256]{1,0:T(8,128)(2,1)}), bf16[1024,1024]{1,0:T(8,128)(2,1)}) %all-gather.26.cloned.1.call-update) | async-done | bytes 2097168 | tf_op jit(solution)/shard_map/all_gather | solution.py:61
  540.9 5.4 fusion.141
  549.6 15.5 %all-gather.32.cloned.1.call-done = bf16[1024,1024]{1,0:T(8,128)(2,1)} async-done(((bf16[1024,256]{1,0:T(8,128)(2,1)}), bf16[1024,1024]{1,0:T(8,128)(2,1)}) %all-gather.32.cloned.1.call-update) | async-done | bytes 2097168 | tf_op jit(solution)/shard_map/all_gather | solution.py:61
  565.1 7.7 multiply_convert_fusion.4
  575.2 3.9 convolution_add_fusion.2
  579.2 44.6 %reduce-scatter.28.cloned.1.call-done = f32[1024,256]{1,0:T(8,128)} async-done(((f32[1024,1024]{1,0:T(8,128)}), f32[1024,256]{1,0:T(8,128)}) %reduce-scatter.28.cloned.1.call-update) | async-done | bytes 1048592 | tf_op jit(solution)/shard_map/reduce_scatter | solution.py:64
  625.5 5.9 all-reduce.8
  635.3 22.9 %all-gather.30.cloned.1.call-done = bf16[1024,1024]{1,0:T(8,128)(2,1)} async-done(((bf16[1024,256]{1,0:T(8,128)(2,1)}), bf16[1024,1024]{1,0:T(8,128)(2,1)}) %all-gather.30.cloned.1.call-update) | async-done | bytes 2097168 | tf_op jit(solution)/shard_map/all_gather | solution.py:61
  663.8 63.1 %while.76 = (s32[]{:T(128)}, bf16[4,1024,64]{1,2,0:T(8,128)(2,1)}, bf16[4,1024,64]{1,2,0:T(8,128)(2,1)}, bf16[4,1024,64]{1,2,0:T(8,128)(2,1)}, s32[1024]{0:T(102...) while((s32[]{:T(128)}, bf16[4,1024,64]{1,2,0:T(8,128)(2,1)}, ...), condition=%wide.region_30.31_spmd.clone, body=%wide.region_27.30_spmd.clone.sunk | while | flops 512721408 | bytes 27057332 | solution.py:225
  726.9 3.4 convolution_convert_fusion
  739.8 63.3 %while.77 = (s32[]{:T(128)}, bf16[4,1024,64]{1,2,0:T(8,128)(2,1)}, bf16[4,1024,64]{1,2,0:T(8,128)(2,1)}, bf16[4,1024,64]{1,2,0:T(8,128)(2,1)}, s32[1024]{0:T(102...) while((s32[]{:T(128)}, bf16[4,1024,64]{1,2,0:T(8,128)(2,1)}, ...), condition=%wide.region_40.41_spmd.clone, body=%wide.region_37.40_spmd.clone.sunk | while | flops 512721408 | bytes 27057332 | solution.py:225
  810.5 5.3 fusion.138
  815.8 5.4 fusion.142
  840.9 3.3 convolution_add_fusion.6
  866.6 21.1 %all-reduce.6 = (f32[1024]{0:T(1024)S(1)}, f32[1024]{0:T(1024)S(1)}) all-reduce(f32[1024]{0:T(1024)S(1)} %add_dynamic-update-slice_fusion.1, f32[1024]{0:T(1024)S(1)} %add_dynamic-update-slice_fusion), channel_id=26, replica_groups=mesh['row'=8,'col'=4] {'row'}, use_global_device_ids=true, to_apply=%region_60.61.clone | all-reduce | flops 2048 | bytes 16384
  887.9 7.3 all-reduce.7
  895.3 6.0 reduce-scatter.18.cloned.1.call-done
  901.2 3.4 fusion.105
  904.6 43.9 %reduce-scatter.22.cloned.1.call-done = f32[1024,256]{1,0:T(8,128)} async-done(((f32[1024,1024]{1,0:T(8,128)}), f32[1024,256]{1,0:T(8,128)}) %reduce-scatter.22.cloned.1.call-update) | async-done | bytes 1048592 | tf_op jit(solution)/shard_map/reduce_scatter | solution.py:64
  954.1 70.7 %reduce-scatter.42.cloned.1.call-done = f32[128,704]{0,1:T(8,128)} async-done(((f32[1024,704]{0,1:T(8,128)}), f32[128,704]{0,1:T(8,128)}) %reduce-scatter.42.cloned.1.call-update) | async-done | bytes 360464 | tf_op jit(solution)/shard_map/reduce_scatter | solution.py:258
  1024.8 75.6 %reduce-scatter.40.cloned.1.call-done = f32[128,704]{0,1:T(8,128)} async-done(((f32[1024,704]{0,1:T(8,128)}), f32[128,704]{0,1:T(8,128)}) %reduce-scatter.40.cloned.1.call-update) | async-done | bytes 360464 | tf_op jit(solution)/shard_map/reduce_scatter | solution.py:257
  1100.4 75.4 %reduce-scatter.44.cloned.1.call-done = f32[704,128]{1,0:T(8,128)} async-done(((f32[704,1024]{1,0:T(8,128)}), f32[704,128]{1,0:T(8,128)}) %reduce-scatter.44.cloned.1.call-update) | async-done | bytes 360464 | tf_op jit(solution)/shard_map/reduce_scatter | solution.py:259
  1175.8 67.1 %reduce-scatter.38.cloned.1.call-done = f32[256,128]{1,0:T(8,128)} async-done(((f32[256,1024]{1,0:T(8,128)}), f32[256,128]{1,0:T(8,128)}) %reduce-scatter.38.cloned.1.call-update) | async-done | bytes 131088 | tf_op jit(solution)/shard_map/reduce_scatter | solution.py:256
  1242.9 66.7 %reduce-scatter.36.cloned.1.call-done = f32[128,256]{1,0:T(8,128)} async-done(((f32[1024,256]{1,0:T(8,128)}), f32[128,256]{1,0:T(8,128)}) %reduce-scatter.36.cloned.1.call-update) | async-done | bytes 131088 | tf_op jit(solution)/shard_map/reduce_scatter | solution.py:255
  1309.6 66.2 %reduce-scatter.34.cloned.1.call-done = f32[128,256]{1,0:T(8,128)} async-done(((f32[1024,256]{1,0:T(8,128)}), f32[128,256]{1,0:T(8,128)}) %reduce-scatter.34.cloned.1.call-update) | async-done | bytes 131088 | tf_op jit(solution)/shard_map/reduce_scatter | solution.py:254
  1375.8 66.7 %reduce-scatter.32.cloned.1.call-done = f32[128,256]{1,0:T(8,128)} async-done(((f32[1024,256]{1,0:T(8,128)}), f32[128,256]{1,0:T(8,128)}) %reduce-scatter.32.cloned.1.call-update) | async-done | bytes 131088 | tf_op jit(solution)/shard_map/reduce_scatter | solution.py:253
  (538 shorter events, 321.8 us)
Async XLA Ops:
  8.0 158.5 %all-gather.14.cloned.1.call-start = ((), (), s32[]{:S(2)}) async-start(), calls=%async_computation.15 | async-start | bytes 2621440 | tf_op jit(solution)/shard_map/all_gather | solution.py:61
  30.4 11.0 copy-start.36
  31.9 41.1 %copy-start.37 = (bf16[128,256]{1,0:T(8,128)(2,1)S(1)}, bf16[128,256]{1,0:T(8,128)(2,1)}, u32[]{:S(2)}) copy-start(bf16[128,256]{1,0:T(8,128)(2,1)} %param.46) | copy-start | bytes 196612
  32.1 9.2 copy-start.44
  37.9 66.6 %copy-start.38 = (bf16[128,256]{1,0:T(8,128)(2,1)S(1)}, bf16[128,256]{1,0:T(8,128)(2,1)}, u32[]{:S(2)}) copy-start(bf16[128,256]{1,0:T(8,128)(2,1)} %param.47) | copy-start | bytes 196612
  37.9 100.0 %copy-start.55 = (s32[2]{0:T(128)S(1)}, s32[2]{0:T(128)}, u32[]{:S(2)}) copy-start(s32[2]{0:T(128)} %param.54) | copy-start | bytes 28
  37.9 100.6 %copy-start.39 = (bf16[256,128]{1,0:T(8,128)(2,1)S(1)}, bf16[256,128]{1,0:T(8,128)(2,1)}, u32[]{:S(2)}) copy-start(bf16[256,128]{1,0:T(8,128)(2,1)} %param.48) | copy-start | bytes 196612
  40.5 177.6 %all-gather.24.cloned.1.call-start = ((), (), s32[]{:S(2)}) async-start(), calls=%async_computation.22 | async-start | bytes 2621440 | tf_op jit(solution)/shard_map/all_gather | solution.py:61
  41.2 245.8 %reduce-scatter.16.cloned.1.call-start = ((), (), s32[]{:S(2)}) async-start(), calls=%async_computation.16 | async-start | bytes 5242880 | tf_op jit(solution)/shard_map/reduce_scatter | solution.py:64
  73.0 96.8 %copy-start.13 = (bf16[1024,256]{1,0:T(8,128)(2,1)}, bf16[1024,256]{1,0:T(8,128)(2,1)S(1)}, u32[]{:S(2)}) copy-start(bf16[1024,256]{1,0:T(8,128)(2,1)S(1)} %all_gather.36) | copy-start | bytes 1572868
  104.5 67.7 %copy-start.17 = (bf16[1024,256]{1,0:T(8,128)(2,1)}, bf16[1024,256]{1,0:T(8,128)(2,1)S(1)}, u32[]{:S(2)}) copy-start(bf16[1024,256]{1,0:T(8,128)(2,1)S(1)} %all_gather.37) | copy-start | bytes 1572868
  217.8 94.9 %reduce-scatter.20.cloned.1.call-start = ((), (), s32[]{:S(2)}) async-start(), calls=%async_computation.23 | async-start | bytes 5242880 | tf_op jit(solution)/shard_map/reduce_scatter | solution.py:64
  270.0 42.7 %copy-start.6 = (bf16[2048,256]{1,0:T(8,128)(2,1)S(1)}, bf16[2048,256]{1,0:T(8,128)(2,1)}, u32[]{:S(2)}) copy-start(bf16[2048,256]{1,0:T(8,128)(2,1)} %param.44) | copy-start | bytes 3145732
  270.1 56.2 %all-gather.18.cloned.1.call-start = ((), (), s32[]{:S(2)}) async-start(), calls=%async_computation.18 | async-start | bytes 1622016 | tf_op jit(solution)/shard_map/all_gather | solution.py:53
  270.6 75.0 %all-gather.16.cloned.1.call-start = ((), (), s32[]{:S(2)}) async-start(), calls=%async_computation.17 | async-start | bytes 2621440 | tf_op jit(solution)/shard_map/all_gather | solution.py:61
  314.6 316.8 %copy-start.8 = (f32[1024,256]{1,0:T(8,128)}, f32[1024,256]{1,0:T(8,128)S(1)}, u32[]{:S(2)}) copy-start(f32[1024,256]{1,0:T(8,128)S(1)} %get-tuple-element.830) | copy-start | bytes 3145732
  314.6 9.8 copy-start.35
  321.7 69.0 %all-gather.20.cloned.1.call-start = ((), (), s32[]{:S(2)}) async-start(), calls=%async_computation.19 | async-start | bytes 1622016 | tf_op jit(solution)/shard_map/all_gather | solution.py:54
  322.2 111.9 %all-gather.22.cloned.1.call-start = ((), (), s32[]{:S(2)}) async-start(), calls=%async_computation.20 | async-start | bytes 1622016 | tf_op jit(solution)/shard_map/all_gather | solution.py:55
  323.0 133.6 %all-gather.28.cloned.1.call-start = ((), (), s32[]{:S(2)}) async-start(), calls=%async_computation.26 | async-start | bytes 2621440 | tf_op jit(solution)/shard_map/all_gather | solution.py:61
  324.3 26.5 %copy-start.50 = (pred[1024]{0:T(1024)(128)(4,1)}, pred[1024]{0:T(1024)(128)(4,1)S(1)}, u32[]{:S(2)}) copy-start(pred[1024]{0:T(1024)(128)(4,1)S(1)} %get-tuple-element.888) | copy-start | bytes 3076
  324.3 26.5 %copy-start.52 = (pred[1024]{0:T(1024)(128)(4,1)}, pred[1024]{0:T(1024)(128)(4,1)S(1)}, u32[]{:S(2)}) copy-start(pred[1024]{0:T(1024)(128)(4,1)S(1)} %get-tuple-element.889) | copy-start | bytes 3076
  325.9 189.2 %reduce-scatter.24.cloned.1.call-start = ((), (), s32[]{:S(2)}) async-start(), calls=%async_computation.27 | async-start | bytes 5242880 | tf_op jit(solution)/shard_map/reduce_scatter | solution.py:64
  456.6 7.6 copy-start.64
  470.6 70.3 %all-gather.26.cloned.1.call-start = ((), (), s32[]{:S(2)}) async-start(), calls=%async_computation.24 | async-start | bytes 2621440 | tf_op jit(solution)/shard_map/all_gather | solution.py:61
  518.1 47.0 %all-gather.32.cloned.1.call-start = ((), (), s32[]{:S(2)}) async-start(), calls=%async_computation.30 | async-start | bytes 2621440 | tf_op jit(solution)/shard_map/all_gather | solution.py:61
  518.7 105.1 %reduce-scatter.28.cloned.1.call-start = ((), (), s32[]{:S(2)}) async-start(), calls=%async_computation.31 | async-start | bytes 5242880 | tf_op jit(solution)/shard_map/reduce_scatter | solution.py:64
  565.1 7.7 copy-start.66
  579.1 79.2 %all-gather.30.cloned.1.call-start = ((), (), s32[]{:S(2)}) async-start(), calls=%async_computation.28 | async-start | bytes 2621440 | tf_op jit(solution)/shard_map/all_gather | solution.py:61
  623.8 7.6 copy-start.10
  634.4 92.5 %all-gather.34.cloned.1.call-start = ((), (), s32[]{:S(2)}) async-start(), calls=%async_computation.32 | async-start | bytes 2621440 | tf_op jit(solution)/shard_map/all_gather | solution.py:61
  635.1 227.9 %reduce-scatter.26.cloned.1.call-start = ((), (), s32[]{:S(2)}) async-start(), calls=%async_computation.29 | async-start | bytes 5242880 | tf_op jit(solution)/shard_map/reduce_scatter | solution.py:64
  737.0 126.1 %reduce-scatter.30.cloned.1.call-start = ((), (), s32[]{:S(2)}) async-start(), calls=%async_computation.33 | async-start | bytes 5242880 | tf_op jit(solution)/shard_map/reduce_scatter | solution.py:64
  809.2 92.0 %reduce-scatter.18.cloned.1.call-start = ((), (), s32[]{:S(2)}) async-start(), calls=%async_computation.21 | async-start | bytes 5242880 | tf_op jit(solution)/shard_map/reduce_scatter | solution.py:64
  815.8 132.7 %reduce-scatter.22.cloned.1.call-start = ((), (), s32[]{:S(2)}) async-start(), calls=%async_computation.25 | async-start | bytes 5242880 | tf_op jit(solution)/shard_map/reduce_scatter | solution.py:64
  821.2 203.6 %reduce-scatter.42.cloned.1.call-start = ((), (), s32[]{:S(2)}) async-start(), calls=%async_computation.39 | async-start | bytes 3244032 | tf_op jit(solution)/shard_map/reduce_scatter | solution.py:258
  829.2 271.2 %reduce-scatter.40.cloned.1.call-start = ((), (), s32[]{:S(2)}) async-start(), calls=%async_computation.38 | async-start | bytes 3244032 | tf_op jit(solution)/shard_map/reduce_scatter | solution.py:257
  836.0 339.7 %reduce-scatter.44.cloned.1.call-start = ((), (), s32[]{:S(2)}) async-start(), calls=%async_computation.40 | async-start | bytes 3244032 | tf_op jit(solution)/shard_map/reduce_scatter | solution.py:259
  844.2 398.7 %reduce-scatter.38.cloned.1.call-start = ((), (), s32[]{:S(2)}) async-start(), calls=%async_computation.37 | async-start | bytes 1179648 | tf_op jit(solution)/shard_map/reduce_scatter | solution.py:256
  849.4 460.2 %reduce-scatter.36.cloned.1.call-start = ((), (), s32[]{:S(2)}) async-start(), calls=%async_computation.36 | async-start | bytes 1179648 | tf_op jit(solution)/shard_map/reduce_scatter | solution.py:255
  853.3 522.6 %reduce-scatter.34.cloned.1.call-start = ((), (), s32[]{:S(2)}) async-start(), calls=%async_computation.35 | async-start | bytes 1179648 | tf_op jit(solution)/shard_map/reduce_scatter | solution.py:254
  857.2 585.4 %reduce-scatter.32.cloned.1.call-start = ((), (), s32[]{:S(2)}) async-start(), calls=%async_computation.34 | async-start | bytes 1179648 | tf_op jit(solution)/shard_map/reduce_scatter | solution.py:253
  863.0 32.2 %copy-start.49 = (f32[1024]{0:T(1024)S(1)}, f32[1024]{0:T(1024)}, u32[]{:S(2)}) copy-start(f32[1024]{0:T(1024)} %copy-done.48) | copy-start | bytes 12292
  863.0 32.2 %copy-start.47 = (f32[1024]{0:T(1024)S(1)}, f32[1024]{0:T(1024)}, u32[]{:S(2)}) copy-start(f32[1024]{0:T(1024)} %copy-done.46) | copy-start | bytes 12292
  863.0 38.2 %copy-start.9 = (f32[1024,256]{1,0:T(8,128)S(1)}, f32[1024,256]{1,0:T(8,128)}, u32[]{:S(2)}) copy-start(f32[1024,256]{1,0:T(8,128)} %copy-done.8) | copy-start | bytes 3145732
  863.0 38.2 %copy-start.53 = (pred[1024]{0:T(1024)(128)(4,1)S(1)}, pred[1024]{0:T(1024)(128)(4,1)}, u32[]{:S(2)}) copy-start(pred[1024]{0:T(1024)(128)(4,1)} %copy-done.52) | copy-start | bytes 3076
  895.2 53.2 %copy-start.51 = (pred[1024]{0:T(1024)(128)(4,1)S(1)}, pred[1024]{0:T(1024)(128)(4,1)}, u32[]{:S(2)}) copy-start(pred[1024]{0:T(1024)(128)(4,1)} %copy-done.50) | copy-start | bytes 3076
  904.6 46.4 %copy-start.34 = (bf16[1024,256]{1,0:T(8,128)(2,1)S(1)}, bf16[1024,256]{1,0:T(8,128)(2,1)}, u32[]{:S(2)}) copy-start(bf16[1024,256]{1,0:T(8,128)(2,1)} %get-tuple-element.874) | copy-start | bytes 1572868
  (55 other events, 142.7 us)
Sparse Core Ops, SparseCore 0:
  40.6 20.3 all-gather.13
  63.1 22.8 all-gather.23
  217.9 42.5 reduce-scatter.15
  270.2 42.4 reduce-scatter.19
  579.3 44.5 reduce-scatter.27
  737.1 44.5 reduce-scatter.25
  809.3 44.3 reduce-scatter.29
  856.3 44.9 reduce-scatter.17
  903.9 44.5 reduce-scatter.21
  952.5 72.3 reduce-scatter.41
  1029.0 71.4 reduce-scatter.39
  1104.4 71.3 reduce-scatter.43
  1179.7 63.1 reduce-scatter.37
  1247.1 62.4 reduce-scatter.35
  1313.5 62.3 reduce-scatter.33
  1380.0 62.4 reduce-scatter.31
Sparse Core Ops, SparseCore 1:
  272.6 41.1 all-gather.17
  321.7 23.8 all-gather.15
  347.5 43.1 all-gather.19
  392.7 41.3 all-gather.21
  435.7 20.9 all-gather.27
  470.7 44.4 reduce-scatter.23
  518.2 22.6 all-gather.25
  542.4 22.7 all-gather.31
  634.5 23.8 all-gather.29
  659.9 22.7 all-gather.33
where the time goes:
time: 1460 us; the launch traced here: 1450 us
  waiting for transfers between devices  837 us (57%)
  matrix products  278 us (19%)
  blocking collectives  209 us (14%)
  other arithmetic  71 us (5%)
  local copies, waits for them, and re-layouts  33.4 us (2%)
  between operations  17.7 us (1%)
    reduce_scatter x8, waiting for transfers between devices, reduce_cols(): lax.psum_scatter(partial_value, 'col', scatter_dimension=1, tiled=True)  165 us
    dot_general x62, matrix products, times_trans(): lax.dot_general(left, right, (((1,), (1,)), ((), ())), preferred_element_...  117 us
    all_gather x8, waiting for transfers between devices, to_full(): return lax.all_gather(values_own, 'col', axis=1, tiled=True)  102 us
    reduce_scatter x1, waiting for transfers between devices, shards(): lax.psum_scatter(local_terms[4], 'row', scatter_dimension=0, tiled=True)  75.6 us
    reduce_scatter x1, waiting for transfers between devices, shards(): lax.psum_scatter(local_terms[6], 'row', scatter_dimension=1, tiled=True)  75.4 us
    reduce_scatter x1, waiting for transfers between devices, shards(): lax.psum_scatter(local_terms[5], 'row', scatter_dimension=0, tiled=True)  70.7 us
    dot_general x46, matrix products, contract_rows(): lax.dot_general(left, right, (((0,), (0,)), ((), ())), preferred_element_...  69.9 us
    reduce_scatter x1, waiting for transfers between devices, shards(): lax.psum_scatter(local_terms[3], 'row', scatter_dimension=1, tiled=True)  67.1 us
  transfers between devices with their start and end apart: 26, of which 19 were waited for; matrix products, arithmetic and copies ran while one was open for 22% of the time, Pallas kernels for 0%

commit v1 on v0

--- a/solution.py
+++ b/solution.py
@@ -6,6 +6,19 @@
 HEAD_DIM = 64
 EPSILON = 1e-06
 MASKED = -1000000000.0
+
+
+def gather_around(x, axis, dim):
+    ways = lax.axis_size(axis)
+    up = [(d, (d + 1) % ways) for d in range(ways)]
+    down = [(d, (d - 1) % ways) for d in range(ways)]
+    earlier, later = ([x], [x])
+    for _ in range(ways // 2):
+        earlier.append(lax.ppermute(earlier[-1], axis, up))
+    for _ in range((ways - 1) // 2):
+        later.append(lax.ppermute(later[-1], axis, down))
+    line = jnp.concatenate([*earlier[::-1], *later[1:]], axis=dim)
+    return jnp.roll(line, (lax.axis_index(axis) - ways // 2) * x.shape[dim], axis=dim)
 
 
 def times_trans(left, right):
@@ -46,7 +59,7 @@
 
     def fetch():
         return (
-            lax.all_gather(w_query, "row", axis=0, tiled=True),
+            gather_around(w_query, "row", 0),
             lax.all_gather(w_key, "row", axis=0, tiled=True),
             lax.all_gather(w_value, "row", axis=0, tiled=True),
             lax.all_gather(w_out, "row", axis=1, tiled=True),

time: 1460 us -> 1450 us (level)
  blocking collectives: 209 us -> 182 us
    all_gather x1 -> x0, blocking collectives: 31.7 us -> none  [fetch(): lax.all_gather(w_query, 'row', axis=0, tiled=True)]
  transfers between devices with their start and end apart: 26 -> 33, of which waited for: 19 -> 21; matrix products, arithmetic and copies ran while one was open for 22% -> 23% of each run, Pallas kernels for 0% -> 0%
where the time goes in v1:
time: 1450 us; the launch traced here: 1440 us
  waiting for transfers between devices  839 us (58%)
  matrix products  278 us (19%)
  blocking collectives  182 us (13%)
  other arithmetic  73.2 us (5%)
  local copies, waits for them, and re-layouts  33.7 us (2%)
  between operations  17.7 us (1%)
  starting transfers between devices  14.8 us (1%)
    reduce_scatter x8, waiting for transfers between devices, reduce_cols(): lax.psum_scatter(partial_value, 'col', scatter_dimension=1, tiled=True)  163 us
    dot_general x62, matrix products, times_trans(): lax.dot_general(left, right, (((1,), (1,)), ((), ())), preferred_element_...  117 us
    all_gather x8, waiting for transfers between devices, to_full(): return lax.all_gather(values_own, 'col', axis=1, tiled=True)  102 us
    reduce_scatter x1, waiting for transfers between devices, shards(): lax.psum_scatter(local_terms[4], 'row', scatter_dimension=0, tiled=True)  75.8 us
    reduce_scatter x1, waiting for transfers between devices, shards(): lax.psum_scatter(local_terms[6], 'row', scatter_dimension=1, tiled=True)  75.5 us
    reduce_scatter x1, waiting for transfers between devices, shards(): lax.psum_scatter(local_terms[5], 'row', scatter_dimension=0, tiled=True)  70.6 us
    dot_general x46, matrix products, contract_rows(): lax.dot_general(left, right, (((0,), (0,)), ((), ())), preferred_element_...  69.9 us
    reduce_scatter x1, waiting for transfers between devices, shards(): lax.psum_scatter(local_terms[3], 'row', scatter_dimension=1, tiled=True)  67.1 us
  transfers between devices with their start and end apart: 33, of which 21 were waited for; matrix products, arithmetic and copies ran while one was open for 23% of the time, Pallas kernels for 0%

profile of v1, /device:TPU:0, one launch (start us, length us, event | category | flops | bytes accessed | tf_op | source)
XLA Modules:
  0.0 1439.0 jit_solution(17949099206993580704)
XLA Ops:
  8.1 22.3 %all-gather = bf16[8,1,128]{2,1,0:T(2,128)(2,1)S(1)} all-gather(bf16[1,1,128]{2,1,0:T(2,128)(2,1)} %bitcast.471), channel_id=1, replica_groups=mesh['row'=8,'col'=4] {'row'}, dimensions={0}, use_global_device_ids=true | all-gather | bytes 2304 | tf_op jit(solution)/shard_map/all_gather | solution.py:69
  32.1 5.7 all-reduce.10
  41.1 4.7 collective-permute-start.4
  45.9 31.4 %all_gather.34 = bf16[1024,256]{1,0:T(8,128)(2,1)S(1)} all-gather(bf16[128,256]{1,0:T(8,128)(2,1)S(1)} %copy-done.35), channel_id=1, replica_groups=mesh['row'=8,'col'=4] {'row'}, dimensions={0}, use_global_device_ids=true | all-gather | bytes 589824 | tf_op jit(solution)/shard_map/all_gather | solution.py:63
  77.5 31.7 %all_gather.35 = bf16[1024,256]{1,0:T(8,128)(2,1)S(1)} all-gather(bf16[128,256]{1,0:T(8,128)(2,1)S(1)} %copy-done.36), channel_id=1, replica_groups=mesh['row'=8,'col'=4] {'row'}, dimensions={0}, use_global_device_ids=true | all-gather | bytes 589824 | tf_op jit(solution)/shard_map/all_gather | solution.py:64
  110.8 28.9 %all_gather.72 = bf16[256,1024]{1,0:T(8,128)(2,1)} all-gather(bf16[256,128]{1,0:T(8,128)(2,1)S(1)} %copy-done.37), channel_id=1, replica_groups=mesh['row'=8,'col'=4] {'row'}, dimensions={1}, use_global_device_ids=true | all-gather | bytes 589824 | tf_op jit(solution)/shard_map/all_gather | solution.py:65
  144.0 3.5 collective-permute-start.6
  151.7 3.4 convolution_convert_fusion.7
  164.3 34.7 %while.74 = (s32[]{:T(128)}, bf16[4,1024,64]{1,2,0:T(8,128)(2,1)}, f32[4,1024]{1,0:T(4,128)S(1)}, s32[1024]{0:T(1024)S(1)}, s32[]{:T(128)}, /*index=5*/bf16[4,10...) while((s32[]{:T(128)}, bf16[4,1024,64]{1,2,0:T(8,128)(2,1)}, ...), condition=%wide.region_7.9_spmd.clone, body=%wide.region_2.8_spmd.clone.sunk | while | flops 209454592 | bytes 10959497 | solution.py:162
  199.0 3.9 fusion.136
  216.5 34.8 %while.75 = (s32[]{:T(128)}, bf16[4,1024,64]{1,2,0:T(8,128)(2,1)}, f32[4,1024]{1,0:T(4,128)S(1)}, s32[1024]{0:T(1024)S(1)}, s32[]{:T(128)}, /*index=5*/bf16[4,10...) while((s32[]{:T(128)}, bf16[4,1024,64]{1,2,0:T(8,128)(2,1)}, ...), condition=%wide.region_19.21_spmd.clone, body=%wide.region_14.20_spmd.clone.sunk | while | flops 209454592 | bytes 10959497 | solution.py:162
  251.2 4.0 fusion.140
  255.9 21.3 %all-gather.1 = bf16[8,1,128]{2,1,0:T(2,128)(2,1)S(1)} all-gather(bf16[1,1,128]{2,1,0:T(2,128)(2,1)S(1)} %bitcast.472), channel_id=1, replica_groups=mesh['row'=8,'col'=4] {'row'}, dimensions={0}, use_global_device_ids=true | all-gather | bytes 2304 | tf_op jit(solution)/shard_map/all_gather | solution.py:70
  277.3 24.5 %reduce-scatter.20.cloned.1.call-done = f32[1024,256]{1,0:T(8,128)} async-done(((f32[1024,1024]{1,0:T(8,128)}), f32[1024,256]{1,0:T(8,128)}) %reduce-scatter.20.cloned.1.call-update) | async-done | bytes 1048592 | tf_op jit(solution)/shard_map/reduce_scatter | solution.py:77
  303.8 6.0 all-reduce.9
  315.4 19.4 %all-gather.16.cloned.1.call-done = bf16[1024,1024]{1,0:T(8,128)(2,1)} async-done(((bf16[1024,256]{1,0:T(8,128)(2,1)}), bf16[1024,1024]{1,0:T(8,128)(2,1)}) %all-gather.16.cloned.1.call-update) | async-done | bytes 2097168 | tf_op jit(solution)/shard_map/all_gather | solution.py:74
  334.8 5.2 fusion.137
  340.0 39.8 %all-gather.20.cloned.1.call-done = bf16[1024,704]{0,1:T(8,128)(2,1)} async-done(((bf16[128,704]{0,1:T(8,128)(2,1)}), bf16[1024,704]{0,1:T(8,128)(2,1)}) %all-gather.20.cloned.1.call-update) | async-done | bytes 1441808 | tf_op jit(solution)/shard_map/all_gather | solution.py:67
  379.8 5.3 fusion.138
  385.1 38.1 %all-gather.22.cloned.1.call-done = bf16[704,1024]{1,0:T(8,128)(2,1)} async-done(((bf16[704,128]{1,0:T(8,128)(2,1)}), bf16[704,1024]{1,0:T(8,128)(2,1)}) %all-gather.22.cloned.1.call-update) | async-done | bytes 1441808 | tf_op jit(solution)/shard_map/all_gather | solution.py:68
  423.3 22.5 %all-gather.28.cloned.1.call-done = bf16[1024,1024]{1,0:T(8,128)(2,1)} async-done(((bf16[1024,256]{1,0:T(8,128)(2,1)}), bf16[1024,1024]{1,0:T(8,128)(2,1)}) %all-gather.28.cloned.1.call-update) | async-done | bytes 2097168 | tf_op jit(solution)/shard_map/all_gather | solution.py:74
  445.8 7.6 multiply_convert_fusion.6
  455.8 3.9 convolution_add_fusion.3
  459.8 44.5 %reduce-scatter.24.cloned.1.call-done = f32[1024,256]{1,0:T(8,128)} async-done(((f32[1024,1024]{1,0:T(8,128)}), f32[1024,256]{1,0:T(8,128)}) %reduce-scatter.24.cloned.1.call-update) | async-done | bytes 1048592 | tf_op jit(solution)/shard_map/reduce_scatter | solution.py:77
  508.1 21.9 %all-gather.26.cloned.1.call-done = bf16[1024,1024]{1,0:T(8,128)(2,1)} async-done(((bf16[1024,256]{1,0:T(8,128)(2,1)}), bf16[1024,1024]{1,0:T(8,128)(2,1)}) %all-gather.26.cloned.1.call-update) | async-done | bytes 2097168 | tf_op jit(solution)/shard_map/all_gather | solution.py:74
  530.1 5.4 fusion.142
  538.8 15.5 %all-gather.32.cloned.1.call-done = bf16[1024,1024]{1,0:T(8,128)(2,1)} async-done(((bf16[1024,256]{1,0:T(8,128)(2,1)}), bf16[1024,1024]{1,0:T(8,128)(2,1)}) %all-gather.32.cloned.1.call-update) | async-done | bytes 2097168 | tf_op jit(solution)/shard_map/all_gather | solution.py:74
  554.3 7.6 multiply_convert_fusion.4
  564.4 3.9 convolution_add_fusion.2
  568.4 44.6 %reduce-scatter.28.cloned.1.call-done = f32[1024,256]{1,0:T(8,128)} async-done(((f32[1024,1024]{1,0:T(8,128)}), f32[1024,256]{1,0:T(8,128)}) %reduce-scatter.28.cloned.1.call-update) | async-done | bytes 1048592 | tf_op jit(solution)/shard_map/reduce_scatter | solution.py:77
  614.7 5.9 all-reduce.8
  624.7 22.7 %all-gather.30.cloned.1.call-done = bf16[1024,1024]{1,0:T(8,128)(2,1)} async-done(((bf16[1024,256]{1,0:T(8,128)(2,1)}), bf16[1024,1024]{1,0:T(8,128)(2,1)}) %all-gather.30.cloned.1.call-update) | async-done | bytes 2097168 | tf_op jit(solution)/shard_map/all_gather | solution.py:74
  653.0 63.0 %while.76 = (s32[]{:T(128)}, bf16[4,1024,64]{1,2,0:T(8,128)(2,1)}, bf16[4,1024,64]{1,2,0:T(8,128)(2,1)}, bf16[4,1024,64]{1,2,0:T(8,128)(2,1)}, s32[1024]{0:T(102...) while((s32[]{:T(128)}, bf16[4,1024,64]{1,2,0:T(8,128)(2,1)}, ...), condition=%wide.region_30.32_spmd.clone, body=%wide.region_27.31_spmd.clone.sunk | while | flops 512721408 | bytes 27057332 | solution.py:238
  728.9 63.3 %while.77 = (s32[]{:T(128)}, bf16[4,1024,64]{1,2,0:T(8,128)(2,1)}, bf16[4,1024,64]{1,2,0:T(8,128)(2,1)}, bf16[4,1024,64]{1,2,0:T(8,128)(2,1)}, s32[1024]{0:T(102...) while((s32[]{:T(128)}, bf16[4,1024,64]{1,2,0:T(8,128)(2,1)}, ...), condition=%wide.region_40.42_spmd.clone, body=%wide.region_37.41_spmd.clone.sunk | while | flops 512721408 | bytes 27057332 | solution.py:238
  799.6 5.3 fusion.139
  804.9 5.4 fusion.143
  855.8 20.9 %all-reduce.6 = (f32[1024]{0:T(1024)S(1)}, f32[1024]{0:T(1024)S(1)}) all-reduce(f32[1024]{0:T(1024)S(1)} %add_dynamic-update-slice_fusion.1, f32[1024]{0:T(1024)S(1)} %add_dynamic-update-slice_fusion), channel_id=26, replica_groups=mesh['row'=8,'col'=4] {'row'}, use_global_device_ids=true, to_apply=%region_60.62.clone | all-reduce | flops 2048 | bytes 16384
  876.9 7.3 all-reduce.7
  884.3 6.0 reduce-scatter.18.cloned.1.call-done
  890.2 3.4 fusion.105
  893.6 43.9 %reduce-scatter.22.cloned.1.call-done = f32[1024,256]{1,0:T(8,128)} async-done(((f32[1024,1024]{1,0:T(8,128)}), f32[1024,256]{1,0:T(8,128)}) %reduce-scatter.22.cloned.1.call-update) | async-done | bytes 1048592 | tf_op jit(solution)/shard_map/reduce_scatter | solution.py:77
  943.1 70.6 %reduce-scatter.42.cloned.1.call-done = f32[128,704]{0,1:T(8,128)} async-done(((f32[1024,704]{0,1:T(8,128)}), f32[128,704]{0,1:T(8,128)}) %reduce-scatter.42.cloned.1.call-update) | async-done | bytes 360464 | tf_op jit(solution)/shard_map/reduce_scatter | solution.py:271
  1013.6 75.8 %reduce-scatter.40.cloned.1.call-done = f32[128,704]{0,1:T(8,128)} async-done(((f32[1024,704]{0,1:T(8,128)}), f32[128,704]{0,1:T(8,128)}) %reduce-scatter.40.cloned.1.call-update) | async-done | bytes 360464 | tf_op jit(solution)/shard_map/reduce_scatter | solution.py:270
  1089.4 75.5 %reduce-scatter.44.cloned.1.call-done = f32[704,128]{1,0:T(8,128)} async-done(((f32[704,1024]{1,0:T(8,128)}), f32[704,128]{1,0:T(8,128)}) %reduce-scatter.44.cloned.1.call-update) | async-done | bytes 360464 | tf_op jit(solution)/shard_map/reduce_scatter | solution.py:272
  1164.9 67.1 %reduce-scatter.38.cloned.1.call-done = f32[256,128]{1,0:T(8,128)} async-done(((f32[256,1024]{1,0:T(8,128)}), f32[256,128]{1,0:T(8,128)}) %reduce-scatter.38.cloned.1.call-update) | async-done | bytes 131088 | tf_op jit(solution)/shard_map/reduce_scatter | solution.py:269
  1232.0 66.6 %reduce-scatter.36.cloned.1.call-done = f32[128,256]{1,0:T(8,128)} async-done(((f32[1024,256]{1,0:T(8,128)}), f32[128,256]{1,0:T(8,128)}) %reduce-scatter.36.cloned.1.call-update) | async-done | bytes 131088 | tf_op jit(solution)/shard_map/reduce_scatter | solution.py:268
  1298.6 66.2 %reduce-scatter.34.cloned.1.call-done = f32[128,256]{1,0:T(8,128)} async-done(((f32[1024,256]{1,0:T(8,128)}), f32[128,256]{1,0:T(8,128)}) %reduce-scatter.34.cloned.1.call-update) | async-done | bytes 131088 | tf_op jit(solution)/shard_map/reduce_scatter | solution.py:267
  1364.9 66.6 %reduce-scatter.32.cloned.1.call-done = f32[128,256]{1,0:T(8,128)} async-done(((f32[1024,256]{1,0:T(8,128)}), f32[128,256]{1,0:T(8,128)}) %reduce-scatter.32.cloned.1.call-update) | async-done | bytes 131088 | tf_op jit(solution)/shard_map/reduce_scatter | solution.py:266
  (558 shorter events, 334.3 us)
Async XLA Ops:
  8.0 33.0 %copy-start.38 = (bf16[128,256]{1,0:T(8,128)(2,1)S(1)}, bf16[128,256]{1,0:T(8,128)(2,1)}, u32[]{:S(2)}) copy-start(bf16[128,256]{1,0:T(8,128)(2,1)} %param.47) | copy-start | bytes 196612
  8.0 143.6 %all-gather.14.cloned.1.call-start = ((), (), s32[]{:S(2)}) async-start(), calls=%async_computation.15 | async-start | bytes 2621440 | tf_op jit(solution)/shard_map/all_gather | solution.py:74
  32.0 45.5 %copy-start.36 = (bf16[128,256]{1,0:T(8,128)(2,1)S(1)}, bf16[128,256]{1,0:T(8,128)(2,1)}, u32[]{:S(2)}) copy-start(bf16[128,256]{1,0:T(8,128)(2,1)} %param.49) | copy-start | bytes 196612
  32.1 45.3 %copy-start.43 = (f32[256]{0:T(256)}, f32[256]{0:T(256)S(1)}, u32[]{:S(2)}) copy-start(f32[256]{0:T(256)S(1)} %dynamic-slice_convert_fusion.1) | copy-start | bytes 3076
  37.9 39.5 %copy-start.39 = (f32[1024]{0:T(1024)}, f32[1024]{0:T(1024)S(1)}, u32[]{:S(2)}) copy-start(f32[1024]{0:T(1024)S(1)} %get-tuple-element.887) | copy-start | bytes 12292
  37.9 39.5 %copy-start.41 = (f32[1024]{0:T(1024)}, f32[1024]{0:T(1024)S(1)}, u32[]{:S(2)}) copy-start(f32[1024]{0:T(1024)S(1)} %get-tuple-element.888) | copy-start | bytes 12292
  38.4 72.4 %copy-start.37 = (bf16[256,128]{1,0:T(8,128)(2,1)S(1)}, bf16[256,128]{1,0:T(8,128)(2,1)}, u32[]{:S(2)}) copy-start(bf16[256,128]{1,0:T(8,128)(2,1)} %param.50) | copy-start | bytes 196612
  38.4 103.4 %copy-start.54 = (s32[2]{0:T(128)S(1)}, s32[2]{0:T(128)}, u32[]{:S(2)}) copy-start(s32[2]{0:T(128)} %param.56) | copy-start | bytes 28
  41.0 162.5 %all-gather.24.cloned.1.call-start = ((), (), s32[]{:S(2)}) async-start(), calls=%async_computation.22 | async-start | bytes 2621440 | tf_op jit(solution)/shard_map/all_gather | solution.py:74
  41.0 36.3 %collective-permute-start = (bf16[128,256]{1,0:T(8,128)(2,1)S(1)}, bf16[128,256]{1,0:T(8,128)(2,1)S(1)}, u32[]{:S(2)}, u32[]{:S(2)}) collective-permute-start(bf16[128,256]{1,0:T(8,128)(2,1)S(1)} %copy-done.38), channel_id=1, source_target_pairs={{0,4},{4,8},{8,12},{12,16},{16,20},{20,24},{24,28},{28,0},{1,5},{5... | collective-permute-start | bytes 196616 | tf_op jit(solution)/shard_map/ppermute | solution.py:17
  41.1 98.6 %collective-permute-start.4 = (bf16[128,256]{1,0:T(8,128)(2,1)S(1)}, bf16[128,256]{1,0:T(8,128)(2,1)S(1)}, u32[]{:S(2)}, u32[]{:S(2)}) collective-permute-start(bf16[128,256]{1,0:T(8,128)(2,1)S(1)} %copy-done.38), channel_id=1, source_target_pairs={{0,28},{4,0},{8,4},{12,8},{16,12},{20,16},{24,20},{28,24},{1,29},{... | collective-permute-start | bytes 196616 | tf_op jit(solution)/shard_map/ppermute | solution.py:19
  45.8 231.5 %reduce-scatter.16.cloned.1.call-start = ((), (), s32[]{:S(2)}) async-start(), calls=%async_computation.16 | async-start | bytes 5242880 | tf_op jit(solution)/shard_map/reduce_scatter | solution.py:77
  77.3 80.0 %copy-start.13 = (bf16[1024,256]{1,0:T(8,128)(2,1)}, bf16[1024,256]{1,0:T(8,128)(2,1)S(1)}, u32[]{:S(2)}) copy-start(bf16[1024,256]{1,0:T(8,128)(2,1)S(1)} %all_gather.34) | copy-start | bytes 1572868
  77.4 31.8 %collective-permute-start.1 = (bf16[128,256]{1,0:T(8,128)(2,1)S(1)}, bf16[128,256]{1,0:T(8,128)(2,1)S(1)}, u32[]{:S(2)}, u32[]{:S(2)}) collective-permute-start(bf16[128,256]{1,0:T(8,128)(2,1)S(1)} %collective-permute-done), channel_id=1, source_target_pairs={{0,4},{4,8},{8,12},{12,16},{16,20},{20,24},{24,28},{28,0},{1,5},{5... | collective-permute-start | bytes 196616 | tf_op jit(solution)/shard_map/ppermute | solution.py:17
  109.2 52.2 %copy-start.16 = (bf16[1024,256]{1,0:T(8,128)(2,1)}, bf16[1024,256]{1,0:T(8,128)(2,1)S(1)}, u32[]{:S(2)}) copy-start(bf16[1024,256]{1,0:T(8,128)(2,1)S(1)} %all_gather.35) | copy-start | bytes 1572868
  109.2 31.4 %collective-permute-start.2 = (bf16[128,256]{1,0:T(8,128)(2,1)S(1)}, bf16[128,256]{1,0:T(8,128)(2,1)S(1)}, u32[]{:S(2)}, u32[]{:S(2)}) collective-permute-start(bf16[128,256]{1,0:T(8,128)(2,1)S(1)} %collective-permute-done.1), channel_id=1, source_target_pairs={{0,4},{4,8},{8,12},{12,16},{16,20},{20,24},{24,28},{28,0},{1,5},{5... | collective-permute-start | bytes 196616 | tf_op jit(solution)/shard_map/ppermute | solution.py:17
  139.7 4.3 collective-permute-start.5
  140.6 7.0 collective-permute-start.3
  144.0 5.4 collective-permute-start.6
  202.9 98.9 %reduce-scatter.20.cloned.1.call-start = ((), (), s32[]{:S(2)}) async-start(), calls=%async_computation.23 | async-start | bytes 5242880 | tf_op jit(solution)/shard_map/reduce_scatter | solution.py:77
  255.2 46.7 %copy-start.6 = (bf16[2048,256]{1,0:T(8,128)(2,1)S(1)}, bf16[2048,256]{1,0:T(8,128)(2,1)}, u32[]{:S(2)}) copy-start(bf16[2048,256]{1,0:T(8,128)(2,1)} %param.46) | copy-start | bytes 3145732
  255.2 60.1 %all-gather.18.cloned.1.call-start = ((), (), s32[]{:S(2)}) async-start(), calls=%async_computation.18 | async-start | bytes 1622016 | tf_op jit(solution)/shard_map/all_gather | solution.py:66
  255.8 79.0 %all-gather.16.cloned.1.call-start = ((), (), s32[]{:S(2)}) async-start(), calls=%async_computation.17 | async-start | bytes 2621440 | tf_op jit(solution)/shard_map/all_gather | solution.py:74
  303.8 316.8 %copy-start.8 = (f32[1024,256]{1,0:T(8,128)}, f32[1024,256]{1,0:T(8,128)S(1)}, u32[]{:S(2)}) copy-start(f32[1024,256]{1,0:T(8,128)S(1)} %get-tuple-element.831) | copy-start | bytes 3145732
  310.8 69.0 %all-gather.20.cloned.1.call-start = ((), (), s32[]{:S(2)}) async-start(), calls=%async_computation.19 | async-start | bytes 1622016 | tf_op jit(solution)/shard_map/all_gather | solution.py:67
  311.4 111.8 %all-gather.22.cloned.1.call-start = ((), (), s32[]{:S(2)}) async-start(), calls=%async_computation.20 | async-start | bytes 1622016 | tf_op jit(solution)/shard_map/all_gather | solution.py:68
  312.1 133.6 %all-gather.28.cloned.1.call-start = ((), (), s32[]{:S(2)}) async-start(), calls=%async_computation.26 | async-start | bytes 2621440 | tf_op jit(solution)/shard_map/all_gather | solution.py:74
  315.1 189.2 %reduce-scatter.24.cloned.1.call-start = ((), (), s32[]{:S(2)}) async-start(), calls=%async_computation.27 | async-start | bytes 5242880 | tf_op jit(solution)/shard_map/reduce_scatter | solution.py:77
  459.8 70.3 %all-gather.26.cloned.1.call-start = ((), (), s32[]{:S(2)}) async-start(), calls=%async_computation.24 | async-start | bytes 2621440 | tf_op jit(solution)/shard_map/all_gather | solution.py:74
  507.3 47.0 %all-gather.32.cloned.1.call-start = ((), (), s32[]{:S(2)}) async-start(), calls=%async_computation.30 | async-start | bytes 2621440 | tf_op jit(solution)/shard_map/all_gather | solution.py:74
  507.9 105.1 %reduce-scatter.28.cloned.1.call-start = ((), (), s32[]{:S(2)}) async-start(), calls=%async_computation.31 | async-start | bytes 5242880 | tf_op jit(solution)/shard_map/reduce_scatter | solution.py:77
  568.3 79.1 %all-gather.30.cloned.1.call-start = ((), (), s32[]{:S(2)}) async-start(), calls=%async_computation.28 | async-start | bytes 2621440 | tf_op jit(solution)/shard_map/all_gather | solution.py:74
  623.5 92.5 %all-gather.34.cloned.1.call-start = ((), (), s32[]{:S(2)}) async-start(), calls=%async_computation.32 | async-start | bytes 2621440 | tf_op jit(solution)/shard_map/all_gather | solution.py:74
  624.3 227.9 %reduce-scatter.26.cloned.1.call-start = ((), (), s32[]{:S(2)}) async-start(), calls=%async_computation.29 | async-start | bytes 5242880 | tf_op jit(solution)/shard_map/reduce_scatter | solution.py:77
  726.1 126.1 %reduce-scatter.30.cloned.1.call-start = ((), (), s32[]{:S(2)}) async-start(), calls=%async_computation.33 | async-start | bytes 5242880 | tf_op jit(solution)/shard_map/reduce_scatter | solution.py:77
  798.3 92.0 %reduce-scatter.18.cloned.1.call-start = ((), (), s32[]{:S(2)}) async-start(), calls=%async_computation.21 | async-start | bytes 5242880 | tf_op jit(solution)/shard_map/reduce_scatter | solution.py:77
  804.9 132.6 %reduce-scatter.22.cloned.1.call-start = ((), (), s32[]{:S(2)}) async-start(), calls=%async_computation.25 | async-start | bytes 5242880 | tf_op jit(solution)/shard_map/reduce_scatter | solution.py:77
  810.4 203.2 %reduce-scatter.42.cloned.1.call-start = ((), (), s32[]{:S(2)}) async-start(), calls=%async_computation.39 | async-start | bytes 3244032 | tf_op jit(solution)/shard_map/reduce_scatter | solution.py:271
  818.4 271.0 %reduce-scatter.40.cloned.1.call-start = ((), (), s32[]{:S(2)}) async-start(), calls=%async_computation.38 | async-start | bytes 3244032 | tf_op jit(solution)/shard_map/reduce_scatter | solution.py:270
  825.2 339.7 %reduce-scatter.44.cloned.1.call-start = ((), (), s32[]{:S(2)}) async-start(), calls=%async_computation.40 | async-start | bytes 3244032 | tf_op jit(solution)/shard_map/reduce_scatter | solution.py:272
  833.4 398.6 %reduce-scatter.38.cloned.1.call-start = ((), (), s32[]{:S(2)}) async-start(), calls=%async_computation.37 | async-start | bytes 1179648 | tf_op jit(solution)/shard_map/reduce_scatter | solution.py:269
  838.6 460.1 %reduce-scatter.36.cloned.1.call-start = ((), (), s32[]{:S(2)}) async-start(), calls=%async_computation.36 | async-start | bytes 1179648 | tf_op jit(solution)/shard_map/reduce_scatter | solution.py:268
  842.4 522.4 %reduce-scatter.34.cloned.1.call-start = ((), (), s32[]{:S(2)}) async-start(), calls=%async_computation.35 | async-start | bytes 1179648 | tf_op jit(solution)/shard_map/reduce_scatter | solution.py:267
  846.4 585.1 %reduce-scatter.32.cloned.1.call-start = ((), (), s32[]{:S(2)}) async-start(), calls=%async_computation.34 | async-start | bytes 1179648 | tf_op jit(solution)/shard_map/reduce_scatter | solution.py:266
  852.1 38.1 %copy-start.9 = (f32[1024,256]{1,0:T(8,128)S(1)}, f32[1024,256]{1,0:T(8,128)}, u32[]{:S(2)}) copy-start(f32[1024,256]{1,0:T(8,128)} %copy-done.8) | copy-start | bytes 3145732
  852.1 38.1 %copy-start.52 = (pred[1024]{0:T(1024)(128)(4,1)S(1)}, pred[1024]{0:T(1024)(128)(4,1)}, u32[]{:S(2)}) copy-start(pred[1024]{0:T(1024)(128)(4,1)} %copy-done.51) | copy-start | bytes 3076
  884.3 53.2 %copy-start.50 = (pred[1024]{0:T(1024)(128)(4,1)S(1)}, pred[1024]{0:T(1024)(128)(4,1)}, u32[]{:S(2)}) copy-start(pred[1024]{0:T(1024)(128)(4,1)} %copy-done.49) | copy-start | bytes 3076
  893.6 46.4 %copy-start.33 = (bf16[1024,256]{1,0:T(8,128)(2,1)S(1)}, bf16[1024,256]{1,0:T(8,128)(2,1)}, u32[]{:S(2)}) copy-start(bf16[1024,256]{1,0:T(8,128)(2,1)} %get-tuple-element.875) | copy-start | bytes 1572868
  (61 other events, 291.6 us)
Sparse Core Ops, SparseCore 0:
  41.1 20.3 all-gather.13
  63.6 22.8 all-gather.23
  203.0 46.4 reduce-scatter.15
  255.3 46.4 reduce-scatter.19
  568.4 44.5 reduce-scatter.27
  726.3 44.5 reduce-scatter.25
  798.4 44.3 reduce-scatter.29
  845.3 44.8 reduce-scatter.17
  892.9 44.5 reduce-scatter.21
  941.4 72.1 reduce-scatter.41
  1017.8 71.5 reduce-scatter.39
  1093.4 71.4 reduce-scatter.43
  1168.9 63.0 reduce-scatter.37
  1236.2 62.3 reduce-scatter.35
  1302.5 62.3 reduce-scatter.33
  1369.1 62.3 reduce-scatter.31
Sparse Core Ops, SparseCore 1:
  257.7 45.1 all-gather.17
  310.9 23.8 all-gather.15
  336.7 43.1 all-gather.19
  381.9 41.3 all-gather.21
  424.8 20.9 all-gather.27
  459.8 44.4 reduce-scatter.23
  507.4 22.7 all-gather.25
  531.6 22.7 all-gather.31
  623.6 23.8 all-gather.29
  649.1 22.7 all-gather.33
